TPU v7x, 256 devices: a whole 4x4x8 slice. The times are simulated.
256 devices in a mesh: tp: 16 (over x, z_lo), hb: 16 (over y, z_hi, core).
Axes of the slice: x: 4, y: 4, z: 8 (z_hi: 2, z_lo: 4; z = z_hi * 4 + z_lo), core: 2. Of those that a mesh axis runs over, the one named last changes fastest.
Arguments:
- normed: bfloat16 [2048, 16384], P('hb', 'tp'), may hold values from -6 to 6
- hidden: bfloat16 [2048, 26624], P('hb', 'tp'), may hold values from -6 to 6
Outputs:
- h_in: float32 [16384, 16384], P('tp', 'hb')
- h_down: float32 [26624, 1664], P(('tp', 'hb'))
All inputs are finite; a program needn't handle non-finite values.
Results may differ from a plain program's by a relative error of at most 0.0003.
Values may be sent and summed in bfloat16 or wider, within the bound.
No kernel may reach another device: no remote copies, remote signals or barrier semaphores. Data moves between devices by JAX's collectives and lax.ppermute only.
A program may use at most 128 MiB of HBM per device.

v0:
```python
import jax
import jax.numpy as jnp
from jax import lax
from jax.sharding import PartitionSpec as P


def gram_product(left, right):
    return lax.dot_general(
        left, right, (((0,), (0,)), ((), ())), preferred_element_type=jnp.float32
    )


def per_device(normed, hidden):
    groups = lax.axis_size("hb")
    scale = 2.0 / (normed.shape[0] * groups)
    whole_rows = lax.all_gather(normed, "tp", axis=1, tiled=True)
    columns = lax.all_to_all(whole_rows, "hb", split_axis=1, concat_axis=0, tiled=True)
    part = columns
    h_in = gram_product(lax.all_gather(normed, "hb", axis=0, tiled=True), part) * scale
    part = hidden
    h_down = (
        lax.psum_scatter(gram_product(part, hidden), "hb", scatter_dimension=0, tiled=True) * scale
    )
    return (h_in, h_down)


def solution(mesh):
    return jax.shard_map(
        per_device,
        mesh=mesh,
        in_specs=(P("hb", "tp"), P("hb", "tp")),
        out_specs=(P("tp", "hb"), P(("tp", "hb"), None)),
        check_vma=False,
    )
```

profile of v0, /device:TPU:2, one launch (start us, length us, event | category | flops | bytes accessed | tf_op | source)
XLA Modules:
  0.0 419.3 jit_solution(16098393865919439729)
XLA Ops:
  7.2 0.0 copy-start
  7.2 0.0 all-gather.5.cloned.1.call-start
  7.2 1.8 copy.6
  9.1 0.0 all-gather.5.cloned.1.call-update
  9.1 0.0 all-gather.3.cloned.1.call-start
  9.1 0.7 all-gather.3.cloned.1.call-update
  9.8 0.0 reduce-scatter.4.cloned.1.call-start
  9.9 0.0 copy-done
  9.9 5.8 %fusion = f32[1664,1664]{1,0:T(8,128)} fusion(bf16[128,1664]{1,0:T(8,128)(2,1)S(1)} %copy-done), kind=kOutput, calls=%fused_computation.2 | convolution fusion | flops 708837376 | bytes 11501568 | tf_op jit(solution)/shard_map/dot_general | solution.py:8
  15.7 0.0 reduce-scatter.4.cloned.1.call-update
  15.8 97.4 %all-gather.5.cloned.1.call-done = bf16[128,16384]{0,1:T(8,128)(2,1)} async-done(((bf16[128,1024]{0,1:T(8,128)(2,1)}), bf16[128,16384]{0,1:T(8,128)(2,1)}) %all-gather.5.cloned.1.call-update) | async-done | bytes 4194320 | tf_op jit(solution)/shard_map/all_gather | solution.py:16
  113.2 134.0 %all_to_all.19 = bf16[128,16,1024]{0,2,1:T(8,128)(2,1)} all-to-all(bf16[128,16,1024]{0,2,1:T(8,128)(2,1)} %bitcast.9), channel_id=1, replica_groups=mesh['tp'=16,'hb'=16] {'hb'}, dimensions={1} | all-to-all | bytes 8388608 | tf_op jit(solution)/shard_map/all_to_all | solution.py:17
  247.1 6.4 %copy.7 = bf16[16,128,1024]{2,1,0:T(8,128)(2,1)} copy(bf16[16,128,1024]{1,2,0:T(8,128)(2,1)} %bitcast.8) | data formatting | bytes 8388608 | tf_op jit(solution)/shard_map/all_to_all | solution.py:17
  253.6 0.0 all-gather.3.cloned.1.call-done
  253.6 10.9 %convolution_multiply_fusion = f32[1024,1024]{1,0:T(8,128)} fusion(bf16[2048,1024]{1,0:T(8,128)(2,1)} %all-gather.3.cloned.1.call-done, bf16[2048,1024]{1,0:T(8,128)(2,1)} %bitcast.10), kind=kOutput, calls=%fused_computation | convolution fusion | flops 4296015872 | bytes 12582912 | tf_op jit(solution)/shard_map/dot_general | solution.py:8
  264.5 146.2 %reduce-scatter.4.cloned.1.call-done = f32[104,1664]{1,0:T(8,128)} async-done(((f32[1664,1664]{1,0:T(8,128)}), f32[104,1664]{1,0:T(8,128)}) %reduce-scatter.4.cloned.1.call-update) | async-done | bytes 692240
  410.8 2.0 broadcast_multiply_fusion
Async XLA Ops:
  7.2 2.7 copy-start
  7.2 106.0 %all-gather.5.cloned.1.call-start = ((), (), s32[]{:S(2)}) async-start(), calls=%async_computation.3 | async-start | bytes 4456448 | tf_op jit(solution)/shard_map/all_gather | solution.py:16
  9.1 244.5 %all-gather.3.cloned.1.call-start = ((), (), s32[]{:S(2)}) async-start(), calls=%async_computation.2 | async-start | bytes 4456448 | tf_op jit(solution)/shard_map/all_gather | solution.py:19
  9.8 400.9 %reduce-scatter.4.cloned.1.call-start = ((), (), s32[]{:S(2)}) async-start(), calls=%async_computation.4 | async-start | bytes 11767808
Sparse Core Ops, SparseCore 0:
  10.4 102.7 all-gather.4
  115.9 106.8 all-gather.2
  227.3 183.4 reduce-scatter.3
where the time goes:
time: 420 us; the launch traced here: 419 us
  waiting for transfers between devices  244 us (58%)
  blocking collectives  134 us (32%)
  matrix products  16.8 us (4%)
  between operations  13.8 us (3%)
  local copies, waits for them, and re-layouts  8.29 us (2%)
    unnamed x4, waiting for transfers between devices  147 us
    all_to_all x1, blocking collectives, per_device(): lax.all_to_all(whole_rows, 'hb', split_axis=1, concat_axis=0, tiled=True)  134 us
    all_gather x1, waiting for transfers between devices, per_device(): whole_rows = lax.all_gather(normed, 'tp', axis=1, tiled=True)  97.4 us
    dot_general x2, matrix products, gram_product(): lax.dot_general(left, right, (((0,), (0,)), ((), ())), preferred_element_...  16.8 us
  transfers between devices with their start and end apart: 3, of which 2 were waited for; matrix products, arithmetic and copies ran while one was open for 6% of the time, Pallas kernels for 0%

commit v1 on v0

--- a/solution.py
+++ b/solution.py
@@ -13,7 +13,9 @@
 def per_device(normed, hidden):
     groups = lax.axis_size("hb")
     scale = 2.0 / (normed.shape[0] * groups)
-    whole_rows = lax.all_gather(normed, "tp", axis=1, tiled=True)
+    whole_rows = jnp.concatenate(
+        lax.all_to_all(jnp.stack([normed] * lax.axis_size("tp")), "tp", 0, 0), axis=1
+    )
     columns = lax.all_to_all(whole_rows, "hb", split_axis=1, concat_axis=0, tiled=True)
     part = columns
     h_in = gram_product(lax.all_gather(normed, "hb", axis=0, tiled=True), part) * scale

time: 420 us -> 363 us (0.86)
  blocking collectives: 134 us -> 0 us
  waiting for transfers between devices: 244 us -> 310 us
  starting transfers between devices: 0.12 us -> 17.5 us
  local copies, waits for them, and re-layouts: 8.29 us -> 3.51 us
    all_to_all x0 -> x2, waiting for transfers between devices: none -> 256 us  [the longest x1 140 us: per_device(): lax.all_to_all(whole_rows, 'hb', split_axis=1, concat_axis=0, tiled=True)]
    all_to_all x1 -> x0, blocking collectives: 134 us -> none  [per_device(): lax.all_to_all(whole_rows, 'hb', split_axis=1, concat_axis=0, tiled=True)]
    all_gather x1 -> x0, waiting for transfers between devices: 97.4 us -> none  [per_device(): whole_rows = lax.all_gather(normed, 'tp', axis=1, tiled=True)]
    unnamed x4 -> x3, waiting for transfers between devices: 147 us -> 53.9 us
    all_to_all x0 -> x2, starting transfers between devices: none -> 17.5 us  [the longest x1 8.91 us: per_device(): lax.all_to_all(jnp.stack([normed] * lax.axis_size('tp')), 'tp', 0, 0)]
    all_to_all x1 -> x0, local copies, waits for them, and re-layouts: 6.45 us -> none  [per_device(): lax.all_to_all(whole_rows, 'hb', split_axis=1, concat_axis=0, tiled=True)]
  transfers between devices with their start and end apart: 3 -> 4, of which waited for: 2 -> 3; matrix products, arithmetic and copies ran while one was open for 6% -> 5% of each run, Pallas kernels for 0% -> 0%
where the time goes in v1:
time: 363 us
  waiting for transfers between devices  310 us (85%)
  starting transfers between devices  17.5 us (5%)
  matrix products  16.2 us (4%)
  between operations  14.1 us (4%)
    all_to_all x1, waiting for transfers between devices, per_device(): lax.all_to_all(whole_rows, 'hb', split_axis=1, concat_axis=0, tiled=True)  140 us
    all_to_all x1, waiting for transfers between devices, per_device(): lax.all_to_all(jnp.stack([normed] * lax.axis_size('tp')), 'tp', 0, 0)  116 us
    unnamed x3, waiting for transfers between devices  53.9 us
    dot_general x2, matrix products, gram_product(): lax.dot_general(left, right, (((0,), (0,)), ((), ())), preferred_element_...  16.2 us
    all_to_all x1, starting transfers between devices, per_device(): lax.all_to_all(jnp.stack([normed] * lax.axis_size('tp')), 'tp', 0, 0)  8.91 us
    all_to_all x1, starting transfers between devices, per_device(): lax.all_to_all(whole_rows, 'hb', split_axis=1, concat_axis=0, tiled=True)  8.55 us
  transfers between devices with their start and end apart: 4, of which 3 were waited for; matrix products, arithmetic and copies ran while one was open for 5% of the time, Pallas kernels for 0%

profile of v1, /device:TPU:2, one launch (start us, length us, event | category | flops | bytes accessed | tf_op | source)
XLA Modules:
  0.0 363.2 jit_solution(1168298404028890197)
XLA Ops:
  7.2 0.0 copy-start
  7.2 0.0 all-gather.2.cloned.1.call-start
  7.2 0.7 all-gather.2.cloned.1.call-update
  7.9 3.5 stack.2
  11.4 8.9 %all-to-all-start = ((bf16[16,128,1024]{2,1,0:T(8,128)(2,1)}), bf16[16,128,1024]{2,1,0:T(8,128)(2,1)}, u32[]{:S(2)}, u32[]{:S(2)}) async-start(bf16[16,128,1024]{2,1,0:T(8,128)(2,1)} %stack.2), calls=%async_computation | async-start | bytes 8388608 | tf_op jit(solution)/shard_map/all_to_all | solution.py:17
  20.3 0.0 reduce-scatter.4.cloned.1.call-start
  20.4 0.0 copy-done
  20.4 5.8 %fusion = f32[1664,1664]{1,0:T(8,128)} fusion(bf16[128,1664]{1,0:T(8,128)(2,1)S(1)} %copy-done), kind=kOutput, calls=%fused_computation.2 | convolution fusion | flops 708837376 | bytes 11501568 | tf_op jit(solution)/shard_map/dot_general | solution.py:8
  26.2 0.0 reduce-scatter.4.cloned.1.call-update
  26.2 115.7 %all-to-all-done = bf16[16,128,1024]{2,1,0:T(8,128)(2,1)} async-done(((bf16[16,128,1024]{2,1,0:T(8,128)(2,1)}), bf16[16,128,1024]{2,1,0:T(8,128)(2,1)}, u32[]{:S(2)}, u32[]{:S(2)}) %all-to-all-start) | async-done | bytes 4194336 | tf_op jit(solution)/shard_map/all_to_all | solution.py:17
  142.0 8.6 %all-to-all-start.1 = ((bf16[128,16,1024]{2,0,1:T(8,128)(2,1)}), bf16[128,16,1024]{2,0,1:T(8,128)(2,1)}, u32[]{:S(2)}, u32[]{:S(2)}) async-start(bf16[128,16,1024]{2,0,1:T(8,128)(2,1)} %bitcast), calls=%async_computation.1 | async-start | bytes 8388608 | tf_op jit(solution)/shard_map/all_to_all | solution.py:19
  150.5 0.0 all-gather.2.cloned.1.call-done
  150.6 140.1 %all-to-all-done.1 = bf16[128,16,1024]{2,0,1:T(8,128)(2,1)} async-done(((bf16[128,16,1024]{2,0,1:T(8,128)(2,1)}), bf16[128,16,1024]{2,0,1:T(8,128)(2,1)}, u32[]{:S(2)}, u32[]{:S(2)}) %all-to-all-start.1) | async-done | bytes 4194336 | tf_op jit(solution)/shard_map/all_to_all | solution.py:19
  290.7 10.4 %convolution_multiply_fusion = f32[1024,1024]{1,0:T(8,128)} fusion(bf16[2048,1024]{1,0:T(8,128)(2,1)} %all-gather.2.cloned.1.call-done, bf16[2048,1024]{1,0:T(8,128)(2,1)} %bitcast.2), kind=kOutput, calls=%fused_computation | convolution fusion | flops 4296015872 | bytes 12582912 | tf_op jit(solution)/shard_map/dot_general | solution.py:8
  301.1 53.2 %reduce-scatter.4.cloned.1.call-done = f32[104,1664]{1,0:T(8,128)} async-done(((f32[1664,1664]{1,0:T(8,128)}), f32[104,1664]{1,0:T(8,128)}) %reduce-scatter.4.cloned.1.call-update) | async-done | bytes 692240
  354.4 2.0 broadcast_multiply_fusion
Async XLA Ops:
  7.2 13.2 %copy-start = (bf16[128,1664]{1,0:T(8,128)(2,1)S(1)}, bf16[128,1664]{1,0:T(8,128)(2,1)}, u32[]{:S(2)}) copy-start(bf16[128,1664]{1,0:T(8,128)(2,1)} %param.3) | copy-start | bytes 1277956
  7.2 143.4 %all-gather.2.cloned.1.call-start = ((), (), s32[]{:S(2)}) async-start(), calls=%async_computation.3 | async-start | bytes 4456448 | tf_op jit(solution)/shard_map/all_gather | solution.py:21
  11.4 130.6 %all-to-all-start = ((bf16[16,128,1024]{2,1,0:T(8,128)(2,1)}), bf16[16,128,1024]{2,1,0:T(8,128)(2,1)}, u32[]{:S(2)}, u32[]{:S(2)}) async-start(bf16[16,128,1024]{2,1,0:T(8,128)(2,1)} %stack.2), calls=%async_computation | async-start | bytes 8388608 | tf_op jit(solution)/shard_map/all_to_all | solution.py:17
  20.3 334.0 %reduce-scatter.4.cloned.1.call-start = ((), (), s32[]{:S(2)}) async-start(), calls=%async_computation.4 | async-start | bytes 11767808
  142.0 148.7 %all-to-all-start.1 = ((bf16[128,16,1024]{2,0,1:T(8,128)(2,1)}), bf16[128,16,1024]{2,0,1:T(8,128)(2,1)}, u32[]{:S(2)}, u32[]{:S(2)}) async-start(bf16[128,16,1024]{2,0,1:T(8,128)(2,1)} %bitcast), calls=%async_computation.1 | async-start | bytes 8388608 | tf_op jit(solution)/shard_map/all_to_all | solution.py:19
Sparse Core Ops, SparseCore 0:
  10.7 82.2 all-gather.1
  97.6 256.7 reduce-scatter.3
